TPU v7x, 256 devices: a whole 4x4x8 slice. The times are simulated.
256 devices in a mesh: tx: 16 (over z, core), gx: 8 (over x, y_lo), gy: 2 (over y_hi).
Axes of the slice: x: 4, y: 4 (y_hi: 2, y_lo: 2; y = y_hi * 2 + y_lo), z: 8, core: 2. Of those that a mesh axis runs over, the one named last changes fastest.
Arguments:
- cond_h: float32 [128, 32, 128], P('gx', 'gy'), may hold values from 0.1 to 1.5
- cond_v: float32 [128, 32, 128], P('gx', 'gy'), may hold values from 0.1 to 1.5
- fwd_init: float32 [16, 6, 128, 32, 128], P('tx', None, 'gx', 'gy'), may hold values from -6 to 6
- adj_init: float32 [16, 6, 128, 32, 128], P('tx', None, 'gx', 'gy'), may hold values from -6 to 6
- observed: float32 [16, 4, 8, 2, 2, 32], P('tx', None, 'gx', 'gy'), may hold values from -6 to 6
- footprint: int32 [16, 8, 2], P('tx', 'gx', 'gy'), may hold values 0 or 1
- owner: int32 [8, 2, 16], P('gx', 'gy'), may hold values from 0 to 15, each once within a row
- rec_cells: int32 [8, 2, 32], P('gx', 'gy'), may hold values from 0 to 255
Outputs:
- owned_gradient: float32 [8, 16, 2, 1, 32, 128], P('gx', 'tx', None, None, 'gy')
- misfit: float32 [], replicated
Inputs may be any that keep to these rules, and one draw needn't show every extreme that they name: `owner`: each tile's row is a permutation of 0 to 15. `rec_cells`: cell index x * 16 + y within the tile; receivers may share a cell. `footprint`: 1 where the group's gradient counts in the tile.
All inputs are finite; a program needn't handle non-finite values.
Results may differ from a plain program's by a relative error of at most 0.00028.
Values sent between devices are 32-bit elements; how exact they have to be, the bound alone decides.
No kernel may reach another device: no remote copies, remote signals or barrier semaphores. Data moves between devices by JAX's collectives and lax.ppermute only.
A program may use at most 64 MiB of HBM per device.

v0:
```python
import jax
import jax.numpy as jnp
from jax import lax
from jax.sharding import PartitionSpec as P

STEPS = 4
ZREC = 32
STEP_DT = 0.5


def shifted(x, axis, by):
    size = lax.axis_size(axis)
    pairs = [(i, i + by) for i in range(size) if 0 <= i + by < size]
    return lax.ppermute(x, axis, pairs)


def coefficients(conduct):
    half_rate = 0.25 * conduct
    return ((1.0 - half_rate) / (1.0 + half_rate), STEP_DT / (1.0 + half_rate))


def ahead_of(values, tail_plane, axis_num):
    extent = values.shape[axis_num]
    return jnp.concatenate(
        [lax.slice_in_dim(values, 1, extent, axis=axis_num), tail_plane], axis=axis_num
    )


def before(values, head_plane, axis_num):
    extent = values.shape[axis_num]
    return jnp.concatenate(
        [head_plane, lax.slice_in_dim(values, 0, extent - 1, axis=axis_num)], axis=axis_num
    )


def zero_plane(values, axis_num):
    return jnp.zeros_like(lax.slice_in_dim(values, 0, 1, axis=axis_num))


def curl_ahead(field, next_x, next_y):
    comp_x, comp_y, comp_z = (field[0], field[1], field[2])
    out_x = (
        ahead_of(comp_z, next_y[1], 1)
        - comp_z
        - (ahead_of(comp_y, zero_plane(comp_y, 2), 2) - comp_y)
    )
    out_y = (
        ahead_of(comp_x, zero_plane(comp_x, 2), 2)
        - comp_x
        - (ahead_of(comp_z, next_x[1], 0) - comp_z)
    )
    out_z = ahead_of(comp_y, next_x[0], 0) - comp_y - (ahead_of(comp_x, next_y[0], 1) - comp_x)
    return jnp.stack([out_x, out_y, out_z])


def curl_before(field, prev_x, prev_y):
    comp_x, comp_y, comp_z = (field[0], field[1], field[2])
    out_x = (
        comp_z - before(comp_z, prev_y[1], 1) - (comp_y - before(comp_y, zero_plane(comp_y, 2), 2))
    )
    out_y = (
        comp_x - before(comp_x, zero_plane(comp_x, 2), 2) - (comp_z - before(comp_z, prev_x[1], 0))
    )
    out_z = comp_y - before(comp_y, prev_x[0], 0) - (comp_x - before(comp_x, prev_y[0], 1))
    return jnp.stack([out_x, out_y, out_z])


def electric_rims(electric):
    next_x = shifted(electric[1:3, 0:1], "gx", -1)
    next_y = shifted(electric[0::2, :, 0:1], "gy", -1)
    return (next_x, next_y)


def magnetic_rims(magnetic):
    size_x = magnetic.shape[1]
    size_y = magnetic.shape[2]
    prev_x = shifted(magnetic[1:3, size_x - 1 : size_x], "gx", 1)
    prev_y = shifted(magnetic[0::2, :, size_y - 1 : size_y], "gy", 1)
    return (prev_x, prev_y)


def advance(electric, magnetic, decay, drive):
    next_x, next_y = electric_rims(electric)
    magnetic = magnetic - STEP_DT * curl_ahead(electric, next_x, next_y)
    prev_x, prev_y = magnetic_rims(magnetic)
    electric = decay * electric + drive * curl_before(magnetic, prev_x, prev_y)
    return (electric, magnetic)


def on_device(cond_h, cond_v, fwd_init, adj_init, observed, footprint, owner, rec_cells):
    size_x, size_y, depth = cond_h.shape
    decay_h, drive_h = coefficients(cond_h)
    decay_v, drive_v = coefficients(cond_v)
    highest = lax.Precision.HIGHEST
    cell_ids = jnp.arange(size_x * size_y, dtype=jnp.int32)
    onehot = (rec_cells[0, 0][:, None] == cell_ids[None, :]).astype(jnp.float32)
    observe = observed[0, :, 0, 0]
    grad_h = jnp.zeros((size_x, size_y, depth), jnp.float32)
    grad_v = jnp.zeros((size_x, size_y, depth), jnp.float32)
    residuals = []
    decay = jnp.stack([decay_h, decay_h, decay_v])
    drive = jnp.stack([drive_h, drive_h, drive_v])
    electric, magnetic = (fwd_init[0, 0:3], fwd_init[0, 3:6])
    stored = []
    for step_idx in range(STEPS):
        electric, magnetic = advance(electric, magnetic, decay, drive)
        stored.append(electric)
        planes = electric[0:2, :, :, ZREC].reshape(2, size_x * size_y)
        residuals.append(jnp.dot(planes, onehot.T, precision=highest) - observe[step_idx])
    adj_e, adj_h = (adj_init[0, 0:3], adj_init[0, 3:6])
    for step_idx in reversed(range(STEPS)):
        adj_e = adj_e.at[0:2, :, :, ZREC].add(
            jnp.dot(residuals[step_idx], onehot, precision=highest).reshape(2, size_x, size_y)
        )
        adj_e, adj_h = advance(adj_e, adj_h, decay, drive)
        kept = stored[step_idx]
        grad_h = grad_h + adj_e[0] * kept[0] + adj_e[1] * kept[1]
        grad_v = grad_v + adj_e[2] * kept[2]
    local_misfit = jnp.float32(0.0)
    for step_idx in range(STEPS):
        local_misfit = local_misfit + 0.5 * jnp.sum(residuals[step_idx] * residuals[step_idx])
    misfit = lax.psum(local_misfit, ("tx", "gx", "gy"))
    tile_flag = footprint[0, 0, 0].astype(jnp.float32)
    gradient = jnp.stack([grad_h, grad_v]) * tile_flag
    groups_count = lax.axis_size("tx")
    block_rows = size_x // groups_count
    blocked = gradient.reshape(2, groups_count, block_rows, size_y, depth)
    ordered = jnp.take(blocked, owner[0, 0], axis=1)
    summed = lax.psum_scatter(ordered, "tx", scatter_dimension=1, tiled=True)
    owned_part = summed.reshape(1, 1, 2, block_rows, size_y, depth)
    return (owned_part, misfit)


def solution(mesh):
    placed = (
        P("gx", "gy", None),
        P("gx", "gy", None),
        P("tx", None, "gx", "gy", None),
        P("tx", None, "gx", "gy", None),
        P("tx", None, "gx", "gy", None, None),
        P("tx", "gx", "gy"),
        P("gx", "gy", None),
        P("gx", "gy", None),
    )
    return jax.shard_map(
        on_device,
        mesh=mesh,
        in_specs=placed,
        out_specs=(P("gx", "tx", None, None, "gy", None), P()),
        check_vma=False,
    )
```

profile of v0, /device:TPU:1, one launch (start us, length us, event | category | flops | bytes accessed | tf_op | source)
XLA Modules:
  0.0 326.6 jit_solution(11279298193173657843)
XLA Ops:
  8.3 1.3 collective-permute-start
  9.6 1.4 collective-permute-start.1
  15.4 2.0 and_reduce_fusion
  19.2 5.6 %collective-permute-start.2 = (f32[2,16,1,128]{3,1,2,0:T(8,128)S(1)}, f32[2,16,1,128]{3,1,2,0:T(8,128)S(1)}, u32[]{:S(2)}, u32[]{:S(2)}) collective-permute-start(f32[2,16,1,128]{3,1,2,0:T(8,128)S(1)} %bitcast.592), channel_id=1, source_target_pairs={{0,1},{2,3},{4,5},{6,7},{8,9},{10,11},{12,13},{14,15},{16,17},{18,... | collective-permute-start | bytes 49160 | tf_op jit(solution)/shard_map/ppermute | solution.py:14
  24.9 4.5 %collective-permute-start.3 = (f32[2,1,16,128]{3,2,1,0:T(8,128)S(1)}, f32[2,1,16,128]{3,2,1,0:T(8,128)S(1)}, u32[]{:S(2)}, u32[]{:S(2)}) collective-permute-start(f32[2,1,16,128]{3,2,1,0:T(8,128)S(1)} %slice.1340), channel_id=1, source_target_pairs={{0,2},{2,4},{4,6},{6,8},{8,10},{10,12},{12,14},{1,3},{3,5},{5,7},{... | collective-permute-start | bytes 49160 | tf_op jit(solution)/shard_map/ppermute | solution.py:14
  32.5 1.3 collective-permute-start.4
  33.8 1.3 collective-permute-start.5
  35.8 1.5 multiply_reduce_fusion.3
  38.5 1.3 collective-permute-done.5
  41.6 6.1 %collective-permute-start.6 = (f32[2,16,1,128]{3,1,2,0:T(8,128)S(1)}, f32[2,16,1,128]{3,1,2,0:T(8,128)S(1)}, u32[]{:S(2)}, u32[]{:S(2)}) collective-permute-start(f32[2,16,1,128]{3,1,2,0:T(8,128)S(1)} %bitcast.593), channel_id=1, source_target_pairs={{0,1},{2,3},{4,5},{6,7},{8,9},{10,11},{12,13},{14,15},{16,17},{18,... | collective-permute-start | bytes 49160 | tf_op jit(solution)/shard_map/ppermute | solution.py:14
  47.8 3.7 %collective-permute-start.7 = (f32[2,1,16,128]{3,2,1,0:T(8,128)S(1)}, f32[2,1,16,128]{3,2,1,0:T(8,128)S(1)}, u32[]{:S(2)}, u32[]{:S(2)}) collective-permute-start(f32[2,1,16,128]{3,2,1,0:T(8,128)S(1)} %slice.1368), channel_id=1, source_target_pairs={{0,2},{2,4},{4,6},{6,8},{8,10},{10,12},{12,14},{1,3},{3,5},{5,7},{... | collective-permute-start | bytes 49160 | tf_op jit(solution)/shard_map/ppermute | solution.py:14
  56.2 1.6 multiply_reduce_fusion.2
  59.1 1.3 collective-permute-start.9
  61.5 2.3 collective-permute-done.8
  68.3 6.1 %collective-permute-start.10 = (f32[2,16,1,128]{3,1,2,0:T(8,128)S(1)}, f32[2,16,1,128]{3,1,2,0:T(8,128)S(1)}, u32[]{:S(2)}, u32[]{:S(2)}) collective-permute-start(f32[2,16,1,128]{3,1,2,0:T(8,128)S(1)} %bitcast.594), channel_id=1, source_target_pairs={{0,1},{2,3},{4,5},{6,7},{8,9},{10,11},{12,13},{14,15},{16,17},{18,... | collective-permute-start | bytes 49160 | tf_op jit(solution)/shard_map/ppermute | solution.py:14
  74.5 3.7 %collective-permute-start.11 = (f32[2,1,16,128]{3,2,1,0:T(8,128)S(1)}, f32[2,1,16,128]{3,2,1,0:T(8,128)S(1)}, u32[]{:S(2)}, u32[]{:S(2)}) collective-permute-start(f32[2,1,16,128]{3,2,1,0:T(8,128)S(1)} %slice.1396), channel_id=1, source_target_pairs={{0,2},{2,4},{4,6},{6,8},{8,10},{10,12},{12,14},{1,3},{3,5},{5,7},{... | collective-permute-start | bytes 49160 | tf_op jit(solution)/shard_map/ppermute | solution.py:14
  84.6 1.5 multiply_reduce_fusion.1
  86.1 1.4 collective-permute-start.12
  87.5 1.3 collective-permute-start.13
  89.6 1.6 reshape.513
  91.2 1.3 collective-permute-done.12
  97.4 5.9 %collective-permute-start.14 = (f32[2,16,1,128]{3,1,2,0:T(8,128)S(1)}, f32[2,16,1,128]{3,1,2,0:T(8,128)S(1)}, u32[]{:S(2)}, u32[]{:S(2)}) collective-permute-start(f32[2,16,1,128]{3,1,2,0:T(8,128)S(1)} %bitcast.595), channel_id=1, source_target_pairs={{0,1},{2,3},{4,5},{6,7},{8,9},{10,11},{12,13},{14,15},{16,17},{18,... | collective-permute-start | bytes 49160 | tf_op jit(solution)/shard_map/ppermute | solution.py:14
  103.3 3.7 %collective-permute-start.15 = (f32[2,1,16,128]{3,2,1,0:T(8,128)S(1)}, f32[2,1,16,128]{3,2,1,0:T(8,128)S(1)}, u32[]{:S(2)}, u32[]{:S(2)}) collective-permute-start(f32[2,1,16,128]{3,2,1,0:T(8,128)S(1)} %slice.1424), channel_id=1, source_target_pairs={{0,2},{2,4},{4,6},{6,8},{8,10},{10,12},{12,14},{1,3},{3,5},{5,7},{... | collective-permute-start | bytes 49160 | tf_op jit(solution)/shard_map/ppermute | solution.py:14
  110.4 1.5 multiply_reduce_fusion
  112.3 2.0 add_select_fusion.3
  114.3 3.6 %scatter-add.14 = f32[3,16,16,128]{3,2,1,0:T(8,128)S(1)} dynamic-update-slice(f32[3,16,16,128]{3,2,1,0:T(8,128)S(1)} %get-tuple-element.51, f32[2,16,16,1]{3,2,1,0:T(8,128)S(1)} %add_select_fusion.3, s32[]{:T(128)} %bitcast.4, s32[]{:T(128)} %constant.106.clone.1, s32[]{:T(128)} %constant.106.clone.1, s32[]{:T(128)} %bitcast.5) | dynamic-update-slice | bytes 4100 | tf_op jit(solution)/shard_map/scatter-add | solution.py:112
  118.0 1.3 collective-permute-start.16
  120.7 3.3 collective-permute-done.16
  126.3 6.1 %collective-permute-start.18 = (f32[2,16,1,128]{3,1,2,0:T(8,128)S(1)}, f32[2,16,1,128]{3,1,2,0:T(8,128)S(1)}, u32[]{:S(2)}, u32[]{:S(2)}) collective-permute-start(f32[2,16,1,128]{3,1,2,0:T(8,128)S(1)} %bitcast.596), channel_id=1, source_target_pairs={{0,1},{2,3},{4,5},{6,7},{8,9},{10,11},{12,13},{14,15},{16,17},{18,... | collective-permute-start | bytes 49160 | tf_op jit(solution)/shard_map/ppermute | solution.py:14
  132.4 3.7 %collective-permute-start.19 = (f32[2,1,16,128]{3,2,1,0:T(8,128)S(1)}, f32[2,1,16,128]{3,2,1,0:T(8,128)S(1)}, u32[]{:S(2)}, u32[]{:S(2)}) collective-permute-start(f32[2,1,16,128]{3,2,1,0:T(8,128)S(1)} %slice.1453), channel_id=1, source_target_pairs={{0,2},{2,4},{4,6},{6,8},{8,10},{10,12},{12,14},{1,3},{3,5},{5,7},{... | collective-permute-start | bytes 49160 | tf_op jit(solution)/shard_map/ppermute | solution.py:14
  138.2 2.0 add_select_fusion.2
  140.3 3.6 %scatter-add.15 = f32[3,16,16,128]{3,2,1,0:T(8,128)S(1)} dynamic-update-slice(f32[3,16,16,128]{3,2,1,0:T(8,128)S(1)} %copy.87, f32[2,16,16,1]{3,2,1,0:T(8,128)S(1)} %add_select_fusion.2, s32[]{:T(128)} %bitcast.4, s32[]{:T(128)} %constant.106.clone.1, s32[]{:T(128)} %constant.106.clone.1, s32[]{:T(128)} %bitcast.5) | dynamic-update-slice | bytes 4100 | tf_op jit(solution)/shard_map/scatter-add | solution.py:112
  145.4 1.3 collective-permute-start.21
  146.7 3.3 collective-permute-done.20
  151.7 6.1 %collective-permute-start.22 = (f32[2,16,1,128]{3,1,2,0:T(8,128)S(1)}, f32[2,16,1,128]{3,1,2,0:T(8,128)S(1)}, u32[]{:S(2)}, u32[]{:S(2)}) collective-permute-start(f32[2,16,1,128]{3,1,2,0:T(8,128)S(1)} %bitcast.597), channel_id=1, source_target_pairs={{0,1},{2,3},{4,5},{6,7},{8,9},{10,11},{12,13},{14,15},{16,17},{18,... | collective-permute-start | bytes 49160 | tf_op jit(solution)/shard_map/ppermute | solution.py:14
  157.8 3.7 %collective-permute-start.23 = (f32[2,1,16,128]{3,2,1,0:T(8,128)S(1)}, f32[2,1,16,128]{3,2,1,0:T(8,128)S(1)}, u32[]{:S(2)}, u32[]{:S(2)}) collective-permute-start(f32[2,1,16,128]{3,2,1,0:T(8,128)S(1)} %slice.1486), channel_id=1, source_target_pairs={{0,2},{2,4},{4,6},{6,8},{8,10},{10,12},{12,14},{1,3},{3,5},{5,7},{... | collective-permute-start | bytes 49160 | tf_op jit(solution)/shard_map/ppermute | solution.py:14
  163.6 2.0 add_select_fusion.1
  165.6 3.6 %scatter-add.16 = f32[3,16,16,128]{3,2,1,0:T(8,128)S(1)} dynamic-update-slice(f32[3,16,16,128]{3,2,1,0:T(8,128)S(1)} %copy.88, f32[2,16,16,1]{3,2,1,0:T(8,128)S(1)} %add_select_fusion.1, s32[]{:T(128)} %bitcast.4, s32[]{:T(128)} %constant.106.clone.1, s32[]{:T(128)} %constant.106.clone.1, s32[]{:T(128)} %bitcast.5) | dynamic-update-slice | bytes 4100 | tf_op jit(solution)/shard_map/scatter-add | solution.py:112
  170.7 1.5 collective-permute-start.25
  172.2 3.1 collective-permute-done.24
  177.5 6.1 %collective-permute-start.26 = (f32[2,16,1,128]{3,1,2,0:T(8,128)S(1)}, f32[2,16,1,128]{3,1,2,0:T(8,128)S(1)}, u32[]{:S(2)}, u32[]{:S(2)}) collective-permute-start(f32[2,16,1,128]{3,1,2,0:T(8,128)S(1)} %bitcast.598), channel_id=1, source_target_pairs={{0,1},{2,3},{4,5},{6,7},{8,9},{10,11},{12,13},{14,15},{16,17},{18,... | collective-permute-start | bytes 49160 | tf_op jit(solution)/shard_map/ppermute | solution.py:14
  183.6 3.7 %collective-permute-start.27 = (f32[2,1,16,128]{3,2,1,0:T(8,128)S(1)}, f32[2,1,16,128]{3,2,1,0:T(8,128)S(1)}, u32[]{:S(2)}, u32[]{:S(2)}) collective-permute-start(f32[2,1,16,128]{3,2,1,0:T(8,128)S(1)} %slice.1517), channel_id=1, source_target_pairs={{0,2},{2,4},{4,6},{6,8},{8,10},{10,12},{12,14},{1,3},{3,5},{5,7},{... | collective-permute-start | bytes 49160 | tf_op jit(solution)/shard_map/ppermute | solution.py:14
  189.6 2.0 add_select_fusion
  191.6 3.6 %scatter-add.19 = f32[3,16,16,128]{3,2,1,0:T(8,128)S(1)} dynamic-update-slice(f32[3,16,16,128]{3,2,1,0:T(8,128)S(1)} %copy.89, f32[2,16,16,1]{3,2,1,0:T(8,128)S(1)} %add_select_fusion, s32[]{:T(128)} %bitcast.4, s32[]{:T(128)} %constant.106.clone.1, s32[]{:T(128)} %constant.106.clone.1, s32[]{:T(128)} %bitcast.5) | dynamic-update-slice | bytes 4100 | tf_op jit(solution)/shard_map/scatter-add | solution.py:112
  198.0 3.3 collective-permute-done.28
  203.1 6.1 %collective-permute-start.30 = (f32[2,16,1,128]{3,1,2,0:T(8,128)S(1)}, f32[2,16,1,128]{3,1,2,0:T(8,128)S(1)}, u32[]{:S(2)}, u32[]{:S(2)}) collective-permute-start(f32[2,16,1,128]{3,1,2,0:T(8,128)S(1)} %bitcast.599), channel_id=1, source_target_pairs={{0,1},{2,3},{4,5},{6,7},{8,9},{10,11},{12,13},{14,15},{16,17},{18,... | collective-permute-start | bytes 49160 | tf_op jit(solution)/shard_map/ppermute | solution.py:14
  209.3 3.7 %collective-permute-start.31 = (f32[2,1,16,128]{3,2,1,0:T(8,128)S(1)}, f32[2,1,16,128]{3,2,1,0:T(8,128)S(1)}, u32[]{:S(2)}, u32[]{:S(2)}) collective-permute-start(f32[2,1,16,128]{3,2,1,0:T(8,128)S(1)} %slice.1548), channel_id=1, source_target_pairs={{0,2},{2,4},{4,6},{6,8},{8,10},{10,12},{12,14},{1,3},{3,5},{5,7},{... | collective-permute-start | bytes 49160 | tf_op jit(solution)/shard_map/ppermute | solution.py:14
  219.5 100.3 %psum.7 = f32[]{:T(128)} all-reduce(f32[]{:T(128)S(6)} %add.229), channel_id=1, replica_groups=mesh['tx'=16,'gx'=8,'gy'=2] {'tx','gx','gy'}, use_global_device_ids=true, to_apply=%region_6.0 | all-reduce | flops 1 | bytes 8 | tf_op jit(solution)/shard_map/psum | solution.py:122
  (413 shorter events, 65.5 us)
Async XLA Ops:
  7.2 3.9 %copy-start = (f32[1,6,16,16,128]{4,3,2,1,0:T(8,128)S(1)}, f32[1,6,16,16,128]{4,3,2,1,0:T(8,128)}, u32[]{:S(2)}) copy-start(f32[1,6,16,16,128]{4,3,2,1,0:T(8,128)} %param.18) | copy-start | bytes 2359300
  7.2 312.6 %reduce-scatter.2.cloned.1.call-start = ((), (), s32[]{:S(2)}) async-start(), calls=%async_computation.1 | async-start | bytes 278528 | tf_op jit(solution)/shard_map/reduce_scatter | solution.py:129
  8.3 10.5 %collective-permute-start = (f32[2,16,1,128]{3,2,1,0:T(1,128)S(1)}, f32[2,16,1,128]{3,2,1,0:T(1,128)S(1)}, u32[]{:S(2)}, u32[]{:S(2)}) collective-permute-start(f32[2,16,1,128]{3,2,1,0:T(1,128)S(1)} %slice.1044), channel_id=1, source_target_pairs={{1,0},{3,2},{5,4},{7,6},{9,8},{11,10},{13,12},{15,14},{17,16},{19,... | collective-permute-start | bytes 49160 | tf_op jit(solution)/shard_map/ppermute | solution.py:14
  9.6 4.3 %copy-start.3 = (f32[1,6,16,16,128]{4,3,2,1,0:T(8,128)S(1)}, f32[1,6,16,16,128]{4,3,2,1,0:T(8,128)}, u32[]{:S(2)}) copy-start(f32[1,6,16,16,128]{4,3,2,1,0:T(8,128)} %param.19) | copy-start | bytes 2359300
  9.6 9.2 %collective-permute-start.1 = (f32[2,1,16,128]{3,2,1,0:T(8,128)S(1)}, f32[2,1,16,128]{3,2,1,0:T(8,128)S(1)}, u32[]{:S(2)}, u32[]{:S(2)}) collective-permute-start(f32[2,1,16,128]{3,2,1,0:T(8,128)S(1)} %slice.1328), channel_id=1, source_target_pairs={{2,0},{4,2},{6,4},{8,6},{10,8},{12,10},{14,12},{3,1},{5,3},{7,5},{... | collective-permute-start | bytes 49160 | tf_op jit(solution)/shard_map/ppermute | solution.py:14
  18.9 21.9 %copy-start.8 = (f32[1,16,16,128]{3,2,1,0:T(8,128)}, f32[1,16,16,128]{3,2,1,0:T(8,128)S(1)}, u32[]{:S(2)}) copy-start(f32[1,16,16,128]{3,2,1,0:T(8,128)S(1)} %fusion.33) | copy-start | bytes 393220
  19.2 10.2 %collective-permute-start.2 = (f32[2,16,1,128]{3,1,2,0:T(8,128)S(1)}, f32[2,16,1,128]{3,1,2,0:T(8,128)S(1)}, u32[]{:S(2)}, u32[]{:S(2)}) collective-permute-start(f32[2,16,1,128]{3,1,2,0:T(8,128)S(1)} %bitcast.592), channel_id=1, source_target_pairs={{0,1},{2,3},{4,5},{6,7},{8,9},{10,11},{12,13},{14,15},{16,17},{18,... | collective-permute-start | bytes 49160 | tf_op jit(solution)/shard_map/ppermute | solution.py:14
  24.9 5.4 %collective-permute-start.3 = (f32[2,1,16,128]{3,2,1,0:T(8,128)S(1)}, f32[2,1,16,128]{3,2,1,0:T(8,128)S(1)}, u32[]{:S(2)}, u32[]{:S(2)}) collective-permute-start(f32[2,1,16,128]{3,2,1,0:T(8,128)S(1)} %slice.1340), channel_id=1, source_target_pairs={{0,2},{2,4},{4,6},{6,8},{8,10},{10,12},{12,14},{1,3},{3,5},{5,7},{... | collective-permute-start | bytes 49160 | tf_op jit(solution)/shard_map/ppermute | solution.py:14
  32.5 6.0 %collective-permute-start.4 = (f32[2,16,1,128]{3,2,1,0:T(1,128)S(1)}, f32[2,16,1,128]{3,2,1,0:T(1,128)S(1)}, u32[]{:S(2)}, u32[]{:S(2)}) collective-permute-start(f32[2,16,1,128]{3,2,1,0:T(1,128)S(1)} %slice.1076), channel_id=1, source_target_pairs={{1,0},{3,2},{5,4},{7,6},{9,8},{11,10},{13,12},{15,14},{17,16},{19,... | collective-permute-start | bytes 49160 | tf_op jit(solution)/shard_map/ppermute | solution.py:14
  33.8 6.0 %collective-permute-start.5 = (f32[2,1,16,128]{3,2,1,0:T(8,128)S(1)}, f32[2,1,16,128]{3,2,1,0:T(8,128)S(1)}, u32[]{:S(2)}, u32[]{:S(2)}) collective-permute-start(f32[2,1,16,128]{3,2,1,0:T(8,128)S(1)} %slice.1355), channel_id=1, source_target_pairs={{2,0},{4,2},{6,4},{8,6},{10,8},{12,10},{14,12},{3,1},{5,3},{7,5},{... | collective-permute-start | bytes 49160 | tf_op jit(solution)/shard_map/ppermute | solution.py:14
  41.6 9.8 %collective-permute-start.6 = (f32[2,16,1,128]{3,1,2,0:T(8,128)S(1)}, f32[2,16,1,128]{3,1,2,0:T(8,128)S(1)}, u32[]{:S(2)}, u32[]{:S(2)}) collective-permute-start(f32[2,16,1,128]{3,1,2,0:T(8,128)S(1)} %bitcast.593), channel_id=1, source_target_pairs={{0,1},{2,3},{4,5},{6,7},{8,9},{10,11},{12,13},{14,15},{16,17},{18,... | collective-permute-start | bytes 49160 | tf_op jit(solution)/shard_map/ppermute | solution.py:14
  47.8 4.5 %collective-permute-start.7 = (f32[2,1,16,128]{3,2,1,0:T(8,128)S(1)}, f32[2,1,16,128]{3,2,1,0:T(8,128)S(1)}, u32[]{:S(2)}, u32[]{:S(2)}) collective-permute-start(f32[2,1,16,128]{3,2,1,0:T(8,128)S(1)} %slice.1368), channel_id=1, source_target_pairs={{0,2},{2,4},{4,6},{6,8},{8,10},{10,12},{12,14},{1,3},{3,5},{5,7},{... | collective-permute-start | bytes 49160 | tf_op jit(solution)/shard_map/ppermute | solution.py:14
  56.2 1.6 copy-start.74
  56.2 2.9 copy-start.72
  57.8 6.0 %collective-permute-start.8 = (f32[2,16,1,128]{3,2,1,0:T(1,128)S(1)}, f32[2,16,1,128]{3,2,1,0:T(1,128)S(1)}, u32[]{:S(2)}, u32[]{:S(2)}) collective-permute-start(f32[2,16,1,128]{3,2,1,0:T(1,128)S(1)} %copy-done.74), channel_id=1, source_target_pairs={{1,0},{3,2},{5,4},{7,6},{9,8},{11,10},{13,12},{15,14},{17,16},{19,... | collective-permute-start | bytes 49160 | tf_op jit(solution)/shard_map/ppermute | solution.py:14
  59.1 5.9 %collective-permute-start.9 = (f32[2,1,16,128]{3,2,1,0:T(8,128)S(1)}, f32[2,1,16,128]{3,2,1,0:T(8,128)S(1)}, u32[]{:S(2)}, u32[]{:S(2)}) collective-permute-start(f32[2,1,16,128]{3,2,1,0:T(8,128)S(1)} %copy-done.72), channel_id=1, source_target_pairs={{2,0},{4,2},{6,4},{8,6},{10,8},{12,10},{14,12},{3,1},{5,3},{7,5},{... | collective-permute-start | bytes 49160 | tf_op jit(solution)/shard_map/ppermute | solution.py:14
  68.3 9.8 %collective-permute-start.10 = (f32[2,16,1,128]{3,1,2,0:T(8,128)S(1)}, f32[2,16,1,128]{3,1,2,0:T(8,128)S(1)}, u32[]{:S(2)}, u32[]{:S(2)}) collective-permute-start(f32[2,16,1,128]{3,1,2,0:T(8,128)S(1)} %bitcast.594), channel_id=1, source_target_pairs={{0,1},{2,3},{4,5},{6,7},{8,9},{10,11},{12,13},{14,15},{16,17},{18,... | collective-permute-start | bytes 49160 | tf_op jit(solution)/shard_map/ppermute | solution.py:14
  74.5 4.5 %collective-permute-start.11 = (f32[2,1,16,128]{3,2,1,0:T(8,128)S(1)}, f32[2,1,16,128]{3,2,1,0:T(8,128)S(1)}, u32[]{:S(2)}, u32[]{:S(2)}) collective-permute-start(f32[2,1,16,128]{3,2,1,0:T(8,128)S(1)} %slice.1396), channel_id=1, source_target_pairs={{0,2},{2,4},{4,6},{6,8},{8,10},{10,12},{12,14},{1,3},{3,5},{5,7},{... | collective-permute-start | bytes 49160 | tf_op jit(solution)/shard_map/ppermute | solution.py:14
  84.6 3.0 copy-start.73
  86.1 2.7 copy-start.80
  86.1 6.4 %collective-permute-start.12 = (f32[2,16,1,128]{3,1,2,0:T(8,128)}, f32[2,16,1,128]{3,1,2,0:T(8,128)}, u32[]{:S(2)}, u32[]{:S(2)}) collective-permute-start(f32[2,16,1,128]{3,1,2,0:T(8,128)} %bitcast.197), channel_id=1, source_target_pairs={{1,0},{3,2},{5,4},{7,6},{9,8},{11,10},{13,12},{15,14},{17,16},{19,... | collective-permute-start | bytes 49160 | tf_op jit(solution)/shard_map/ppermute | solution.py:14
  87.5 5.7 %collective-permute-start.13 = (f32[2,1,16,128]{3,2,1,0:T(8,128)S(1)}, f32[2,1,16,128]{3,2,1,0:T(8,128)}, u32[]{:S(2)}, u32[]{:S(2)}) collective-permute-start(f32[2,1,16,128]{3,2,1,0:T(8,128)S(1)} %copy-done.73), channel_id=1, source_target_pairs={{2,0},{4,2},{6,4},{8,6},{10,8},{12,10},{14,12},{3,1},{5,3},{7,5},{... | collective-permute-start | bytes 49160 | tf_op jit(solution)/shard_map/ppermute | solution.py:14
  97.4 9.6 %collective-permute-start.14 = (f32[2,16,1,128]{3,1,2,0:T(8,128)S(1)}, f32[2,16,1,128]{3,1,2,0:T(8,128)S(1)}, u32[]{:S(2)}, u32[]{:S(2)}) collective-permute-start(f32[2,16,1,128]{3,1,2,0:T(8,128)S(1)} %bitcast.595), channel_id=1, source_target_pairs={{0,1},{2,3},{4,5},{6,7},{8,9},{10,11},{12,13},{14,15},{16,17},{18,... | collective-permute-start | bytes 49160 | tf_op jit(solution)/shard_map/ppermute | solution.py:14
  103.3 4.5 %collective-permute-start.15 = (f32[2,1,16,128]{3,2,1,0:T(8,128)S(1)}, f32[2,1,16,128]{3,2,1,0:T(8,128)S(1)}, u32[]{:S(2)}, u32[]{:S(2)}) collective-permute-start(f32[2,1,16,128]{3,2,1,0:T(8,128)S(1)} %slice.1424), channel_id=1, source_target_pairs={{0,2},{2,4},{4,6},{6,8},{8,10},{10,12},{12,14},{1,3},{3,5},{5,7},{... | collective-permute-start | bytes 49160 | tf_op jit(solution)/shard_map/ppermute | solution.py:14
  109.1 1.3 copy-start.81
  110.0 2.2 copy-start.62
  118.0 6.0 %collective-permute-start.16 = (f32[2,16,1,128]{3,1,2,0:T(8,128)S(1)}, f32[2,16,1,128]{3,1,2,0:T(8,128)S(1)}, u32[]{:S(2)}, u32[]{:S(2)}) collective-permute-start(f32[2,16,1,128]{3,1,2,0:T(8,128)S(1)} %bitcast.589), channel_id=1, source_target_pairs={{1,0},{3,2},{5,4},{7,6},{9,8},{11,10},{13,12},{15,14},{17,16},{19,... | collective-permute-start | bytes 49160 | tf_op jit(solution)/shard_map/ppermute | solution.py:14
  119.4 5.5 %collective-permute-start.17 = (f32[2,1,16,128]{3,2,1,0:T(8,128)S(1)}, f32[2,1,16,128]{3,2,1,0:T(8,128)S(1)}, u32[]{:S(2)}, u32[]{:S(2)}) collective-permute-start(f32[2,1,16,128]{3,2,1,0:T(8,128)S(1)} %slice.1440), channel_id=1, source_target_pairs={{2,0},{4,2},{6,4},{8,6},{10,8},{12,10},{14,12},{3,1},{5,3},{7,5},{... | collective-permute-start | bytes 49160 | tf_op jit(solution)/shard_map/ppermute | solution.py:14
  126.3 9.8 %collective-permute-start.18 = (f32[2,16,1,128]{3,1,2,0:T(8,128)S(1)}, f32[2,16,1,128]{3,1,2,0:T(8,128)S(1)}, u32[]{:S(2)}, u32[]{:S(2)}) collective-permute-start(f32[2,16,1,128]{3,1,2,0:T(8,128)S(1)} %bitcast.596), channel_id=1, source_target_pairs={{0,1},{2,3},{4,5},{6,7},{8,9},{10,11},{12,13},{14,15},{16,17},{18,... | collective-permute-start | bytes 49160 | tf_op jit(solution)/shard_map/ppermute | solution.py:14
  132.4 4.5 %collective-permute-start.19 = (f32[2,1,16,128]{3,2,1,0:T(8,128)S(1)}, f32[2,1,16,128]{3,2,1,0:T(8,128)S(1)}, u32[]{:S(2)}, u32[]{:S(2)}) collective-permute-start(f32[2,1,16,128]{3,2,1,0:T(8,128)S(1)} %slice.1453), channel_id=1, source_target_pairs={{0,2},{2,4},{4,6},{6,8},{8,10},{10,12},{12,14},{1,3},{3,5},{5,7},{... | collective-permute-start | bytes 49160 | tf_op jit(solution)/shard_map/ppermute | solution.py:14
  143.9 6.0 %collective-permute-start.20 = (f32[2,16,1,128]{3,1,2,0:T(8,128)S(1)}, f32[2,16,1,128]{3,1,2,0:T(8,128)S(1)}, u32[]{:S(2)}, u32[]{:S(2)}) collective-permute-start(f32[2,16,1,128]{3,1,2,0:T(8,128)S(1)} %bitcast.590), channel_id=1, source_target_pairs={{1,0},{3,2},{5,4},{7,6},{9,8},{11,10},{13,12},{15,14},{17,16},{19,... | collective-permute-start | bytes 49160 | tf_op jit(solution)/shard_map/ppermute | solution.py:14
  145.4 4.7 %collective-permute-start.21 = (f32[2,1,16,128]{3,2,1,0:T(8,128)S(1)}, f32[2,1,16,128]{3,2,1,0:T(8,128)S(1)}, u32[]{:S(2)}, u32[]{:S(2)}) collective-permute-start(f32[2,1,16,128]{3,2,1,0:T(8,128)S(1)} %slice.1473), channel_id=1, source_target_pairs={{2,0},{4,2},{6,4},{8,6},{10,8},{12,10},{14,12},{3,1},{5,3},{7,5},{... | collective-permute-start | bytes 49160 | tf_op jit(solution)/shard_map/ppermute | solution.py:14
  150.2 1.3 copy-start.5
  151.7 9.8 %collective-permute-start.22 = (f32[2,16,1,128]{3,1,2,0:T(8,128)S(1)}, f32[2,16,1,128]{3,1,2,0:T(8,128)S(1)}, u32[]{:S(2)}, u32[]{:S(2)}) collective-permute-start(f32[2,16,1,128]{3,1,2,0:T(8,128)S(1)} %bitcast.597), channel_id=1, source_target_pairs={{0,1},{2,3},{4,5},{6,7},{8,9},{10,11},{12,13},{14,15},{16,17},{18,... | collective-permute-start | bytes 49160 | tf_op jit(solution)/shard_map/ppermute | solution.py:14
  157.8 4.5 %collective-permute-start.23 = (f32[2,1,16,128]{3,2,1,0:T(8,128)S(1)}, f32[2,1,16,128]{3,2,1,0:T(8,128)S(1)}, u32[]{:S(2)}, u32[]{:S(2)}) collective-permute-start(f32[2,1,16,128]{3,2,1,0:T(8,128)S(1)} %slice.1486), channel_id=1, source_target_pairs={{0,2},{2,4},{4,6},{6,8},{8,10},{10,12},{12,14},{1,3},{3,5},{5,7},{... | collective-permute-start | bytes 49160 | tf_op jit(solution)/shard_map/ppermute | solution.py:14
  169.3 6.0 %collective-permute-start.24 = (f32[2,16,1,128]{3,1,2,0:T(8,128)S(1)}, f32[2,16,1,128]{3,1,2,0:T(8,128)S(1)}, u32[]{:S(2)}, u32[]{:S(2)}) collective-permute-start(f32[2,16,1,128]{3,1,2,0:T(8,128)S(1)} %bitcast.591), channel_id=1, source_target_pairs={{1,0},{3,2},{5,4},{7,6},{9,8},{11,10},{13,12},{15,14},{17,16},{19,... | collective-permute-start | bytes 49160 | tf_op jit(solution)/shard_map/ppermute | solution.py:14
  170.7 5.0 %collective-permute-start.25 = (f32[2,1,16,128]{3,2,1,0:T(8,128)S(1)}, f32[2,1,16,128]{3,2,1,0:T(8,128)S(1)}, u32[]{:S(2)}, u32[]{:S(2)}) collective-permute-start(f32[2,1,16,128]{3,2,1,0:T(8,128)S(1)} %slice.1504), channel_id=1, source_target_pairs={{2,0},{4,2},{6,4},{8,6},{10,8},{12,10},{14,12},{3,1},{5,3},{7,5},{... | collective-permute-start | bytes 49160 | tf_op jit(solution)/shard_map/ppermute | solution.py:14
  176.0 1.3 copy-start.39
  176.1 1.3 copy-start.50
  176.1 1.3 copy-start.52
  177.5 9.8 %collective-permute-start.26 = (f32[2,16,1,128]{3,1,2,0:T(8,128)S(1)}, f32[2,16,1,128]{3,1,2,0:T(8,128)S(1)}, u32[]{:S(2)}, u32[]{:S(2)}) collective-permute-start(f32[2,16,1,128]{3,1,2,0:T(8,128)S(1)} %bitcast.598), channel_id=1, source_target_pairs={{0,1},{2,3},{4,5},{6,7},{8,9},{10,11},{12,13},{14,15},{16,17},{18,... | collective-permute-start | bytes 49160 | tf_op jit(solution)/shard_map/ppermute | solution.py:14
  183.6 4.5 %collective-permute-start.27 = (f32[2,1,16,128]{3,2,1,0:T(8,128)S(1)}, f32[2,1,16,128]{3,2,1,0:T(8,128)S(1)}, u32[]{:S(2)}, u32[]{:S(2)}) collective-permute-start(f32[2,1,16,128]{3,2,1,0:T(8,128)S(1)} %slice.1517), channel_id=1, source_target_pairs={{0,2},{2,4},{4,6},{6,8},{8,10},{10,12},{12,14},{1,3},{3,5},{5,7},{... | collective-permute-start | bytes 49160 | tf_op jit(solution)/shard_map/ppermute | solution.py:14
  195.3 6.0 %collective-permute-start.28 = (f32[2,16,1,128]{3,2,1,0:T(1,128)S(1)}, f32[2,16,1,128]{3,2,1,0:T(1,128)S(1)}, u32[]{:S(2)}, u32[]{:S(2)}) collective-permute-start(f32[2,16,1,128]{3,2,1,0:T(1,128)S(1)} %slice.1285), channel_id=1, source_target_pairs={{1,0},{3,2},{5,4},{7,6},{9,8},{11,10},{13,12},{15,14},{17,16},{19,... | collective-permute-start | bytes 49160 | tf_op jit(solution)/shard_map/ppermute | solution.py:14
  196.7 4.7 %collective-permute-start.29 = (f32[2,1,16,128]{3,2,1,0:T(8,128)S(1)}, f32[2,1,16,128]{3,2,1,0:T(8,128)S(1)}, u32[]{:S(2)}, u32[]{:S(2)}) collective-permute-start(f32[2,1,16,128]{3,2,1,0:T(8,128)S(1)} %slice.1535), channel_id=1, source_target_pairs={{2,0},{4,2},{6,4},{8,6},{10,8},{12,10},{14,12},{3,1},{5,3},{7,5},{... | collective-permute-start | bytes 49160 | tf_op jit(solution)/shard_map/ppermute | solution.py:14
  201.5 1.2 copy-start.7
  201.7 1.3 copy-start.51
  203.1 9.8 %collective-permute-start.30 = (f32[2,16,1,128]{3,1,2,0:T(8,128)S(1)}, f32[2,16,1,128]{3,1,2,0:T(8,128)S(1)}, u32[]{:S(2)}, u32[]{:S(2)}) collective-permute-start(f32[2,16,1,128]{3,1,2,0:T(8,128)S(1)} %bitcast.599), channel_id=1, source_target_pairs={{0,1},{2,3},{4,5},{6,7},{8,9},{10,11},{12,13},{14,15},{16,17},{18,... | collective-permute-start | bytes 49160 | tf_op jit(solution)/shard_map/ppermute | solution.py:14
  209.3 4.5 %collective-permute-start.31 = (f32[2,1,16,128]{3,2,1,0:T(8,128)S(1)}, f32[2,1,16,128]{3,2,1,0:T(8,128)S(1)}, u32[]{:S(2)}, u32[]{:S(2)}) collective-permute-start(f32[2,1,16,128]{3,2,1,0:T(8,128)S(1)} %slice.1548), channel_id=1, source_target_pairs={{0,2},{2,4},{4,6},{6,8},{8,10},{10,12},{12,14},{1,3},{3,5},{5,7},{... | collective-permute-start | bytes 49160 | tf_op jit(solution)/shard_map/ppermute | solution.py:14
  (67 other events, 65.3 us)
Sparse Core Ops, SparseCore 0:
  217.1 75.4 reduce-scatter.1
where the time goes:
time: 329 us; the launch traced here: 327 us
  blocking collectives  100 us (30%)
  starting transfers between devices  99.3 us (30%)
  local copies, waits for them, and re-layouts  54.1 us (16%)
  waiting for transfers between devices  27.5 us (8%)
  between operations  19.4 us (6%)
  other arithmetic  18.6 us (6%)
  matrix products  7.47 us (2%)
    psum x1, blocking collectives, on_device(): misfit = lax.psum(local_misfit, ('tx', 'gx', 'gy'))  100 us
    ppermute x32, starting transfers between devices, shifted(): return lax.ppermute(x, axis, pairs)  99.2 us
    ppermute x32, waiting for transfers between devices, shifted(): return lax.ppermute(x, axis, pairs)  27.5 us
    unnamed x167, local copies, waits for them, and re-layouts  21.2 us
    scatter-add x4, local copies, waits for them, and re-layouts, on_device(): adj_e.at[0:2, :, :, ZREC]  14.4 us
    another operation x6, other arithmetic  10.1 us
  transfers between devices with their start and end apart: 33, of which 20 were waited for; matrix products, arithmetic and copies ran while one was open for 4% of the time, Pallas kernels for 0%

commit v1 on v0

--- a/solution.py
+++ b/solution.py
@@ -6,6 +6,11 @@
 STEPS = 4
 ZREC = 32
 STEP_DT = 0.5
+
+
+def by_each_axis(value, inner_axis, outer_axis):
+    partial = lax.psum(value, inner_axis)
+    return lax.psum(partial, outer_axis)
 
 
 def shifted(x, axis, by):
@@ -119,7 +124,7 @@
     local_misfit = jnp.float32(0.0)
     for step_idx in range(STEPS):
         local_misfit = local_misfit + 0.5 * jnp.sum(residuals[step_idx] * residuals[step_idx])
-    misfit = lax.psum(local_misfit, ("tx", "gx", "gy"))
+    misfit = by_each_axis(local_misfit, ("gx", "gy"), "tx")
     tile_flag = footprint[0, 0, 0].astype(jnp.float32)
     gradient = jnp.stack([grad_h, grad_v]) * tile_flag
     groups_count = lax.axis_size("tx")

time: 329 us -> 316 us (0.960)
  blocking collectives: 100 us -> 84.4 us
    psum x1 -> x2, blocking collectives: 100 us -> 84.4 us  [the longest x1 53.3 us: by_each_axis(): return lax.psum(partial, outer_axis)]
where the time goes in v1:
time: 316 us; the launch traced here: 314 us
  starting transfers between devices  99.1 us (31%)
  blocking collectives  84.4 us (27%)
  local copies, waits for them, and re-layouts  56 us (18%)
  waiting for transfers between devices  27.7 us (9%)
  other arithmetic  19.8 us (6%)
  between operations  19.3 us (6%)
  matrix products  7.44 us (2%)
    ppermute x32, starting transfers between devices, shifted(): return lax.ppermute(x, axis, pairs)  99.1 us
    psum x1, blocking collectives, by_each_axis(): return lax.psum(partial, outer_axis)  53.3 us
    psum x1, blocking collectives, by_each_axis(): partial = lax.psum(value, inner_axis)  31.1 us
    ppermute x32, waiting for transfers between devices, shifted(): return lax.ppermute(x, axis, pairs)  27.6 us
    unnamed x167, local copies, waits for them, and re-layouts  21.2 us
    scatter-add x4, local copies, waits for them, and re-layouts, on_device(): adj_e.at[0:2, :, :, ZREC]  16.3 us
    another operation x6, other arithmetic  11.3 us
  transfers between devices with their start and end apart: 33, of which 20 were waited for; matrix products, arithmetic and copies ran while one was open for 4% of the time, Pallas kernels for 0%

profile of v1, /device:TPU:1, one launch (start us, length us, event | category | flops | bytes accessed | tf_op | source)
XLA Modules:
  0.0 313.7 jit_solution(6891984223829156185)
XLA Ops:
  8.3 1.3 collective-permute-start
  9.6 1.4 collective-permute-start.1
  15.4 1.9 and_reduce_fusion
  19.1 5.6 %collective-permute-start.2 = (f32[2,16,1,128]{3,1,2,0:T(8,128)S(1)}, f32[2,16,1,128]{3,1,2,0:T(8,128)S(1)}, u32[]{:S(2)}, u32[]{:S(2)}) collective-permute-start(f32[2,16,1,128]{3,1,2,0:T(8,128)S(1)} %bitcast.592), channel_id=1, source_target_pairs={{0,1},{2,3},{4,5},{6,7},{8,9},{10,11},{12,13},{14,15},{16,17},{18,... | collective-permute-start | bytes 49160 | tf_op jit(solution)/shard_map/ppermute | solution.py:19
  24.8 4.5 %collective-permute-start.3 = (f32[2,1,16,128]{3,2,1,0:T(8,128)S(1)}, f32[2,1,16,128]{3,2,1,0:T(8,128)S(1)}, u32[]{:S(2)}, u32[]{:S(2)}) collective-permute-start(f32[2,1,16,128]{3,2,1,0:T(8,128)S(1)} %slice.1340), channel_id=1, source_target_pairs={{0,2},{2,4},{4,6},{6,8},{8,10},{10,12},{12,14},{1,3},{3,5},{5,7},{... | collective-permute-start | bytes 49160 | tf_op jit(solution)/shard_map/ppermute | solution.py:19
  32.4 1.3 collective-permute-start.4
  33.7 1.3 collective-permute-start.5
  35.8 1.5 multiply_reduce_fusion.3
  38.4 1.3 collective-permute-done.5
  41.6 6.1 %collective-permute-start.6 = (f32[2,16,1,128]{3,1,2,0:T(8,128)S(1)}, f32[2,16,1,128]{3,1,2,0:T(8,128)S(1)}, u32[]{:S(2)}, u32[]{:S(2)}) collective-permute-start(f32[2,16,1,128]{3,1,2,0:T(8,128)S(1)} %bitcast.593), channel_id=1, source_target_pairs={{0,1},{2,3},{4,5},{6,7},{8,9},{10,11},{12,13},{14,15},{16,17},{18,... | collective-permute-start | bytes 49160 | tf_op jit(solution)/shard_map/ppermute | solution.py:19
  47.7 3.7 %collective-permute-start.7 = (f32[2,1,16,128]{3,2,1,0:T(8,128)S(1)}, f32[2,1,16,128]{3,2,1,0:T(8,128)S(1)}, u32[]{:S(2)}, u32[]{:S(2)}) collective-permute-start(f32[2,1,16,128]{3,2,1,0:T(8,128)S(1)} %slice.1368), channel_id=1, source_target_pairs={{0,2},{2,4},{4,6},{6,8},{8,10},{10,12},{12,14},{1,3},{3,5},{5,7},{... | collective-permute-start | bytes 49160 | tf_op jit(solution)/shard_map/ppermute | solution.py:19
  56.2 1.6 multiply_reduce_fusion.2
  59.0 1.3 collective-permute-start.9
  61.4 2.3 collective-permute-done.8
  68.3 6.1 %collective-permute-start.10 = (f32[2,16,1,128]{3,1,2,0:T(8,128)S(1)}, f32[2,16,1,128]{3,1,2,0:T(8,128)S(1)}, u32[]{:S(2)}, u32[]{:S(2)}) collective-permute-start(f32[2,16,1,128]{3,1,2,0:T(8,128)S(1)} %bitcast.594), channel_id=1, source_target_pairs={{0,1},{2,3},{4,5},{6,7},{8,9},{10,11},{12,13},{14,15},{16,17},{18,... | collective-permute-start | bytes 49160 | tf_op jit(solution)/shard_map/ppermute | solution.py:19
  74.4 3.7 %collective-permute-start.11 = (f32[2,1,16,128]{3,2,1,0:T(8,128)S(1)}, f32[2,1,16,128]{3,2,1,0:T(8,128)S(1)}, u32[]{:S(2)}, u32[]{:S(2)}) collective-permute-start(f32[2,1,16,128]{3,2,1,0:T(8,128)S(1)} %slice.1396), channel_id=1, source_target_pairs={{0,2},{2,4},{4,6},{6,8},{8,10},{10,12},{12,14},{1,3},{3,5},{5,7},{... | collective-permute-start | bytes 49160 | tf_op jit(solution)/shard_map/ppermute | solution.py:19
  84.5 1.5 multiply_reduce_fusion.1
  86.1 1.4 collective-permute-start.12
  87.5 1.3 collective-permute-start.13
  89.6 1.6 reshape.513
  91.1 1.3 collective-permute-done.12
  97.4 5.9 %collective-permute-start.14 = (f32[2,16,1,128]{3,1,2,0:T(8,128)S(1)}, f32[2,16,1,128]{3,1,2,0:T(8,128)S(1)}, u32[]{:S(2)}, u32[]{:S(2)}) collective-permute-start(f32[2,16,1,128]{3,1,2,0:T(8,128)S(1)} %bitcast.595), channel_id=1, source_target_pairs={{0,1},{2,3},{4,5},{6,7},{8,9},{10,11},{12,13},{14,15},{16,17},{18,... | collective-permute-start | bytes 49160 | tf_op jit(solution)/shard_map/ppermute | solution.py:19
  103.3 3.7 %collective-permute-start.15 = (f32[2,1,16,128]{3,2,1,0:T(8,128)S(1)}, f32[2,1,16,128]{3,2,1,0:T(8,128)S(1)}, u32[]{:S(2)}, u32[]{:S(2)}) collective-permute-start(f32[2,1,16,128]{3,2,1,0:T(8,128)S(1)} %slice.1424), channel_id=1, source_target_pairs={{0,2},{2,4},{4,6},{6,8},{8,10},{10,12},{12,14},{1,3},{3,5},{5,7},{... | collective-permute-start | bytes 49160 | tf_op jit(solution)/shard_map/ppermute | solution.py:19
  110.3 1.5 multiply_reduce_fusion
  112.2 2.0 add_select_fusion.3
  114.2 3.6 %scatter-add.14 = f32[3,16,16,128]{3,2,1,0:T(8,128)S(1)} dynamic-update-slice(f32[3,16,16,128]{3,2,1,0:T(8,128)S(1)} %get-tuple-element.51, f32[2,16,16,1]{3,2,1,0:T(8,128)S(1)} %add_select_fusion.3, s32[]{:T(128)} %bitcast.4, s32[]{:T(128)} %constant.106.clone.1, s32[]{:T(128)} %constant.106.clone.1, s32[]{:T(128)} %bitcast.5) | dynamic-update-slice | bytes 4100 | tf_op jit(solution)/shard_map/scatter-add | solution.py:117
  119.3 1.3 collective-permute-start.17
  120.6 3.3 %collective-permute-done.16 = f32[2,16,1,128]{3,1,2,0:T(8,128)S(1)} collective-permute-done((f32[2,16,1,128]{3,1,2,0:T(8,128)S(1)}, f32[2,16,1,128]{3,1,2,0:T(8,128)S(1)}, u32[]{:S(2)}, u32[]{:S(2)}) %collective-permute-start.16) | collective-permute-done | bytes 16416 | tf_op jit(solution)/shard_map/ppermute | solution.py:19
  126.2 6.1 %collective-permute-start.18 = (f32[2,16,1,128]{3,1,2,0:T(8,128)S(1)}, f32[2,16,1,128]{3,1,2,0:T(8,128)S(1)}, u32[]{:S(2)}, u32[]{:S(2)}) collective-permute-start(f32[2,16,1,128]{3,1,2,0:T(8,128)S(1)} %bitcast.596), channel_id=1, source_target_pairs={{0,1},{2,3},{4,5},{6,7},{8,9},{10,11},{12,13},{14,15},{16,17},{18,... | collective-permute-start | bytes 49160 | tf_op jit(solution)/shard_map/ppermute | solution.py:19
  132.3 3.7 %collective-permute-start.19 = (f32[2,1,16,128]{3,2,1,0:T(8,128)S(1)}, f32[2,1,16,128]{3,2,1,0:T(8,128)S(1)}, u32[]{:S(2)}, u32[]{:S(2)}) collective-permute-start(f32[2,1,16,128]{3,2,1,0:T(8,128)S(1)} %slice.1453), channel_id=1, source_target_pairs={{0,2},{2,4},{4,6},{6,8},{8,10},{10,12},{12,14},{1,3},{3,5},{5,7},{... | collective-permute-start | bytes 49160 | tf_op jit(solution)/shard_map/ppermute | solution.py:19
  138.2 2.0 add_select_fusion.2
  140.1 3.6 %scatter-add.15 = f32[3,16,16,128]{3,2,1,0:T(8,128)S(1)} dynamic-update-slice(f32[3,16,16,128]{3,2,1,0:T(8,128)S(1)} %copy.87, f32[2,16,16,1]{3,2,1,0:T(8,128)S(1)} %add_select_fusion.2, s32[]{:T(128)} %bitcast.4, s32[]{:T(128)} %constant.106.clone.1, s32[]{:T(128)} %constant.106.clone.1, s32[]{:T(128)} %bitcast.5) | dynamic-update-slice | bytes 4100 | tf_op jit(solution)/shard_map/scatter-add | solution.py:117
  146.5 3.3 %collective-permute-done.20 = f32[2,16,1,128]{3,1,2,0:T(8,128)S(1)} collective-permute-done((f32[2,16,1,128]{3,1,2,0:T(8,128)S(1)}, f32[2,16,1,128]{3,1,2,0:T(8,128)S(1)}, u32[]{:S(2)}, u32[]{:S(2)}) %collective-permute-start.20) | collective-permute-done | bytes 16416 | tf_op jit(solution)/shard_map/ppermute | solution.py:19
  151.5 6.1 %collective-permute-start.22 = (f32[2,16,1,128]{3,1,2,0:T(8,128)S(1)}, f32[2,16,1,128]{3,1,2,0:T(8,128)S(1)}, u32[]{:S(2)}, u32[]{:S(2)}) collective-permute-start(f32[2,16,1,128]{3,1,2,0:T(8,128)S(1)} %bitcast.597), channel_id=1, source_target_pairs={{0,1},{2,3},{4,5},{6,7},{8,9},{10,11},{12,13},{14,15},{16,17},{18,... | collective-permute-start | bytes 49160 | tf_op jit(solution)/shard_map/ppermute | solution.py:19
  157.7 3.7 %collective-permute-start.23 = (f32[2,1,16,128]{3,2,1,0:T(8,128)S(1)}, f32[2,1,16,128]{3,2,1,0:T(8,128)S(1)}, u32[]{:S(2)}, u32[]{:S(2)}) collective-permute-start(f32[2,1,16,128]{3,2,1,0:T(8,128)S(1)} %slice.1486), channel_id=1, source_target_pairs={{0,2},{2,4},{4,6},{6,8},{8,10},{10,12},{12,14},{1,3},{3,5},{5,7},{... | collective-permute-start | bytes 49160 | tf_op jit(solution)/shard_map/ppermute | solution.py:19
  163.5 2.7 add_select_fusion.1
  166.2 4.5 %scatter-add.16 = f32[3,16,16,128]{3,2,1,0:T(8,128)S(1)} dynamic-update-slice(f32[3,16,16,128]{3,2,1,0:T(8,128)S(1)} %copy.88, f32[2,16,16,1]{3,2,1,0:T(8,128)} %add_select_fusion.1, s32[]{:T(128)} %bitcast.4, s32[]{:T(128)} %constant.106.clone.1, s32[]{:T(128)} %constant.106.clone.1, s32[]{:T(128)} %bitcast.5) | dynamic-update-slice | bytes 4100 | tf_op jit(solution)/shard_map/scatter-add | solution.py:117
  172.2 1.5 collective-permute-start.25
  173.7 3.1 collective-permute-done.24
  178.9 6.1 %collective-permute-start.26 = (f32[2,16,1,128]{3,1,2,0:T(8,128)S(1)}, f32[2,16,1,128]{3,1,2,0:T(8,128)S(1)}, u32[]{:S(2)}, u32[]{:S(2)}) collective-permute-start(f32[2,16,1,128]{3,1,2,0:T(8,128)S(1)} %bitcast.598), channel_id=1, source_target_pairs={{0,1},{2,3},{4,5},{6,7},{8,9},{10,11},{12,13},{14,15},{16,17},{18,... | collective-permute-start | bytes 49160 | tf_op jit(solution)/shard_map/ppermute | solution.py:19
  185.1 3.7 %collective-permute-start.27 = (f32[2,1,16,128]{3,2,1,0:T(8,128)S(1)}, f32[2,1,16,128]{3,2,1,0:T(8,128)S(1)}, u32[]{:S(2)}, u32[]{:S(2)}) collective-permute-start(f32[2,1,16,128]{3,2,1,0:T(8,128)S(1)} %slice.1517), channel_id=1, source_target_pairs={{0,2},{2,4},{4,6},{6,8},{8,10},{10,12},{12,14},{1,3},{3,5},{5,7},{... | collective-permute-start | bytes 49160 | tf_op jit(solution)/shard_map/ppermute | solution.py:19
  191.0 2.7 add_select_fusion
  193.7 4.5 %scatter-add.19 = f32[3,16,16,128]{3,2,1,0:T(8,128)S(1)} dynamic-update-slice(f32[3,16,16,128]{3,2,1,0:T(8,128)S(1)} %copy.89, f32[2,16,16,1]{3,2,1,0:T(8,128)} %add_select_fusion, s32[]{:T(128)} %bitcast.4, s32[]{:T(128)} %constant.106.clone.1, s32[]{:T(128)} %constant.106.clone.1, s32[]{:T(128)} %bitcast.5) | dynamic-update-slice | bytes 4100 | tf_op jit(solution)/shard_map/scatter-add | solution.py:117
  201.0 3.3 %collective-permute-done.28 = f32[2,16,1,128]{3,2,1,0:T(1,128)S(1)} collective-permute-done((f32[2,16,1,128]{3,2,1,0:T(1,128)S(1)}, f32[2,16,1,128]{3,2,1,0:T(1,128)S(1)}, u32[]{:S(2)}, u32[]{:S(2)}) %collective-permute-start.28) | collective-permute-done | bytes 16416 | tf_op jit(solution)/shard_map/ppermute | solution.py:19
  206.4 5.9 %collective-permute-start.30 = (f32[2,16,1,128]{3,1,2,0:T(8,128)S(1)}, f32[2,16,1,128]{3,1,2,0:T(8,128)S(1)}, u32[]{:S(2)}, u32[]{:S(2)}) collective-permute-start(f32[2,16,1,128]{3,1,2,0:T(8,128)S(1)} %bitcast.599), channel_id=1, source_target_pairs={{0,1},{2,3},{4,5},{6,7},{8,9},{10,11},{12,13},{14,15},{16,17},{18,... | collective-permute-start | bytes 49160 | tf_op jit(solution)/shard_map/ppermute | solution.py:19
  212.3 3.7 %collective-permute-start.31 = (f32[2,1,16,128]{3,2,1,0:T(8,128)S(1)}, f32[2,1,16,128]{3,2,1,0:T(8,128)S(1)}, u32[]{:S(2)}, u32[]{:S(2)}) collective-permute-start(f32[2,1,16,128]{3,2,1,0:T(8,128)S(1)} %slice.1548), channel_id=1, source_target_pairs={{0,2},{2,4},{4,6},{6,8},{8,10},{10,12},{12,14},{1,3},{3,5},{5,7},{... | collective-permute-start | bytes 49160 | tf_op jit(solution)/shard_map/ppermute | solution.py:19
  222.5 31.1 %psum.14 = f32[]{:T(128)} all-reduce(f32[]{:T(128)S(6)} %add.231), channel_id=1, replica_groups=mesh['tx'=16,'gx'=8,'gy'=2] {'gx','gy'}, use_global_device_ids=true, to_apply=%region_6.0 | all-reduce | flops 1 | bytes 8 | tf_op jit(solution)/shard_map/psum | solution.py:12
  253.5 53.3 %psum.15 = f32[]{:T(128)} all-reduce(f32[]{:T(128)} %psum.14), channel_id=1, replica_groups=mesh['tx'=16,'gx'=8,'gy'=2] {'tx'}, use_global_device_ids=true, to_apply=%region_7.0 | all-reduce | flops 1 | bytes 8 | tf_op jit(solution)/shard_map/psum | solution.py:13
  (414 shorter events, 67.0 us)
Async XLA Ops:
  7.2 3.9 %copy-start = (f32[1,6,16,16,128]{4,3,2,1,0:T(8,128)S(1)}, f32[1,6,16,16,128]{4,3,2,1,0:T(8,128)}, u32[]{:S(2)}) copy-start(f32[1,6,16,16,128]{4,3,2,1,0:T(8,128)} %param.18) | copy-start | bytes 2359300
  7.2 299.7 %reduce-scatter.2.cloned.1.call-start = ((), (), s32[]{:S(2)}) async-start(), calls=%async_computation.1 | async-start | bytes 278528 | tf_op jit(solution)/shard_map/reduce_scatter | solution.py:134
  8.3 10.5 %collective-permute-start = (f32[2,16,1,128]{3,2,1,0:T(1,128)S(1)}, f32[2,16,1,128]{3,2,1,0:T(1,128)S(1)}, u32[]{:S(2)}, u32[]{:S(2)}) collective-permute-start(f32[2,16,1,128]{3,2,1,0:T(1,128)S(1)} %slice.1044), channel_id=1, source_target_pairs={{1,0},{3,2},{5,4},{7,6},{9,8},{11,10},{13,12},{15,14},{17,16},{19,... | collective-permute-start | bytes 49160 | tf_op jit(solution)/shard_map/ppermute | solution.py:19
  9.6 4.3 %copy-start.3 = (f32[1,6,16,16,128]{4,3,2,1,0:T(8,128)S(1)}, f32[1,6,16,16,128]{4,3,2,1,0:T(8,128)}, u32[]{:S(2)}) copy-start(f32[1,6,16,16,128]{4,3,2,1,0:T(8,128)} %param.19) | copy-start | bytes 2359300
  9.6 9.2 %collective-permute-start.1 = (f32[2,1,16,128]{3,2,1,0:T(8,128)S(1)}, f32[2,1,16,128]{3,2,1,0:T(8,128)S(1)}, u32[]{:S(2)}, u32[]{:S(2)}) collective-permute-start(f32[2,1,16,128]{3,2,1,0:T(8,128)S(1)} %slice.1328), channel_id=1, source_target_pairs={{2,0},{4,2},{6,4},{8,6},{10,8},{12,10},{14,12},{3,1},{5,3},{7,5},{... | collective-permute-start | bytes 49160 | tf_op jit(solution)/shard_map/ppermute | solution.py:19
  18.9 21.9 %copy-start.8 = (f32[1,16,16,128]{3,2,1,0:T(8,128)}, f32[1,16,16,128]{3,2,1,0:T(8,128)S(1)}, u32[]{:S(2)}) copy-start(f32[1,16,16,128]{3,2,1,0:T(8,128)S(1)} %fusion.33) | copy-start | bytes 393220
  19.1 10.2 %collective-permute-start.2 = (f32[2,16,1,128]{3,1,2,0:T(8,128)S(1)}, f32[2,16,1,128]{3,1,2,0:T(8,128)S(1)}, u32[]{:S(2)}, u32[]{:S(2)}) collective-permute-start(f32[2,16,1,128]{3,1,2,0:T(8,128)S(1)} %bitcast.592), channel_id=1, source_target_pairs={{0,1},{2,3},{4,5},{6,7},{8,9},{10,11},{12,13},{14,15},{16,17},{18,... | collective-permute-start | bytes 49160 | tf_op jit(solution)/shard_map/ppermute | solution.py:19
  24.8 5.4 %collective-permute-start.3 = (f32[2,1,16,128]{3,2,1,0:T(8,128)S(1)}, f32[2,1,16,128]{3,2,1,0:T(8,128)S(1)}, u32[]{:S(2)}, u32[]{:S(2)}) collective-permute-start(f32[2,1,16,128]{3,2,1,0:T(8,128)S(1)} %slice.1340), channel_id=1, source_target_pairs={{0,2},{2,4},{4,6},{6,8},{8,10},{10,12},{12,14},{1,3},{3,5},{5,7},{... | collective-permute-start | bytes 49160 | tf_op jit(solution)/shard_map/ppermute | solution.py:19
  32.4 6.0 %collective-permute-start.4 = (f32[2,16,1,128]{3,2,1,0:T(1,128)S(1)}, f32[2,16,1,128]{3,2,1,0:T(1,128)S(1)}, u32[]{:S(2)}, u32[]{:S(2)}) collective-permute-start(f32[2,16,1,128]{3,2,1,0:T(1,128)S(1)} %slice.1076), channel_id=1, source_target_pairs={{1,0},{3,2},{5,4},{7,6},{9,8},{11,10},{13,12},{15,14},{17,16},{19,... | collective-permute-start | bytes 49160 | tf_op jit(solution)/shard_map/ppermute | solution.py:19
  33.7 6.0 %collective-permute-start.5 = (f32[2,1,16,128]{3,2,1,0:T(8,128)S(1)}, f32[2,1,16,128]{3,2,1,0:T(8,128)S(1)}, u32[]{:S(2)}, u32[]{:S(2)}) collective-permute-start(f32[2,1,16,128]{3,2,1,0:T(8,128)S(1)} %slice.1355), channel_id=1, source_target_pairs={{2,0},{4,2},{6,4},{8,6},{10,8},{12,10},{14,12},{3,1},{5,3},{7,5},{... | collective-permute-start | bytes 49160 | tf_op jit(solution)/shard_map/ppermute | solution.py:19
  41.6 9.8 %collective-permute-start.6 = (f32[2,16,1,128]{3,1,2,0:T(8,128)S(1)}, f32[2,16,1,128]{3,1,2,0:T(8,128)S(1)}, u32[]{:S(2)}, u32[]{:S(2)}) collective-permute-start(f32[2,16,1,128]{3,1,2,0:T(8,128)S(1)} %bitcast.593), channel_id=1, source_target_pairs={{0,1},{2,3},{4,5},{6,7},{8,9},{10,11},{12,13},{14,15},{16,17},{18,... | collective-permute-start | bytes 49160 | tf_op jit(solution)/shard_map/ppermute | solution.py:19
  47.7 4.5 %collective-permute-start.7 = (f32[2,1,16,128]{3,2,1,0:T(8,128)S(1)}, f32[2,1,16,128]{3,2,1,0:T(8,128)S(1)}, u32[]{:S(2)}, u32[]{:S(2)}) collective-permute-start(f32[2,1,16,128]{3,2,1,0:T(8,128)S(1)} %slice.1368), channel_id=1, source_target_pairs={{0,2},{2,4},{4,6},{6,8},{8,10},{10,12},{12,14},{1,3},{3,5},{5,7},{... | collective-permute-start | bytes 49160 | tf_op jit(solution)/shard_map/ppermute | solution.py:19
  56.2 1.6 copy-start.74
  56.2 2.9 copy-start.72
  57.7 6.0 %collective-permute-start.8 = (f32[2,16,1,128]{3,2,1,0:T(1,128)S(1)}, f32[2,16,1,128]{3,2,1,0:T(1,128)S(1)}, u32[]{:S(2)}, u32[]{:S(2)}) collective-permute-start(f32[2,16,1,128]{3,2,1,0:T(1,128)S(1)} %copy-done.74), channel_id=1, source_target_pairs={{1,0},{3,2},{5,4},{7,6},{9,8},{11,10},{13,12},{15,14},{17,16},{19,... | collective-permute-start | bytes 49160 | tf_op jit(solution)/shard_map/ppermute | solution.py:19
  59.0 5.9 %collective-permute-start.9 = (f32[2,1,16,128]{3,2,1,0:T(8,128)S(1)}, f32[2,1,16,128]{3,2,1,0:T(8,128)S(1)}, u32[]{:S(2)}, u32[]{:S(2)}) collective-permute-start(f32[2,1,16,128]{3,2,1,0:T(8,128)S(1)} %copy-done.72), channel_id=1, source_target_pairs={{2,0},{4,2},{6,4},{8,6},{10,8},{12,10},{14,12},{3,1},{5,3},{7,5},{... | collective-permute-start | bytes 49160 | tf_op jit(solution)/shard_map/ppermute | solution.py:19
  68.3 9.8 %collective-permute-start.10 = (f32[2,16,1,128]{3,1,2,0:T(8,128)S(1)}, f32[2,16,1,128]{3,1,2,0:T(8,128)S(1)}, u32[]{:S(2)}, u32[]{:S(2)}) collective-permute-start(f32[2,16,1,128]{3,1,2,0:T(8,128)S(1)} %bitcast.594), channel_id=1, source_target_pairs={{0,1},{2,3},{4,5},{6,7},{8,9},{10,11},{12,13},{14,15},{16,17},{18,... | collective-permute-start | bytes 49160 | tf_op jit(solution)/shard_map/ppermute | solution.py:19
  74.4 4.5 %collective-permute-start.11 = (f32[2,1,16,128]{3,2,1,0:T(8,128)S(1)}, f32[2,1,16,128]{3,2,1,0:T(8,128)S(1)}, u32[]{:S(2)}, u32[]{:S(2)}) collective-permute-start(f32[2,1,16,128]{3,2,1,0:T(8,128)S(1)} %slice.1396), channel_id=1, source_target_pairs={{0,2},{2,4},{4,6},{6,8},{8,10},{10,12},{12,14},{1,3},{3,5},{5,7},{... | collective-permute-start | bytes 49160 | tf_op jit(solution)/shard_map/ppermute | solution.py:19
  84.5 2.9 copy-start.73
  86.1 2.7 copy-start.80
  86.1 6.4 %collective-permute-start.12 = (f32[2,16,1,128]{3,1,2,0:T(8,128)}, f32[2,16,1,128]{3,1,2,0:T(8,128)}, u32[]{:S(2)}, u32[]{:S(2)}) collective-permute-start(f32[2,16,1,128]{3,1,2,0:T(8,128)} %bitcast.197), channel_id=1, source_target_pairs={{1,0},{3,2},{5,4},{7,6},{9,8},{11,10},{13,12},{15,14},{17,16},{19,... | collective-permute-start | bytes 49160 | tf_op jit(solution)/shard_map/ppermute | solution.py:19
  87.5 5.7 %collective-permute-start.13 = (f32[2,1,16,128]{3,2,1,0:T(8,128)S(1)}, f32[2,1,16,128]{3,2,1,0:T(8,128)}, u32[]{:S(2)}, u32[]{:S(2)}) collective-permute-start(f32[2,1,16,128]{3,2,1,0:T(8,128)S(1)} %copy-done.73), channel_id=1, source_target_pairs={{2,0},{4,2},{6,4},{8,6},{10,8},{12,10},{14,12},{3,1},{5,3},{7,5},{... | collective-permute-start | bytes 49160 | tf_op jit(solution)/shard_map/ppermute | solution.py:19
  97.4 9.6 %collective-permute-start.14 = (f32[2,16,1,128]{3,1,2,0:T(8,128)S(1)}, f32[2,16,1,128]{3,1,2,0:T(8,128)S(1)}, u32[]{:S(2)}, u32[]{:S(2)}) collective-permute-start(f32[2,16,1,128]{3,1,2,0:T(8,128)S(1)} %bitcast.595), channel_id=1, source_target_pairs={{0,1},{2,3},{4,5},{6,7},{8,9},{10,11},{12,13},{14,15},{16,17},{18,... | collective-permute-start | bytes 49160 | tf_op jit(solution)/shard_map/ppermute | solution.py:19
  103.3 4.5 %collective-permute-start.15 = (f32[2,1,16,128]{3,2,1,0:T(8,128)S(1)}, f32[2,1,16,128]{3,2,1,0:T(8,128)S(1)}, u32[]{:S(2)}, u32[]{:S(2)}) collective-permute-start(f32[2,1,16,128]{3,2,1,0:T(8,128)S(1)} %slice.1424), channel_id=1, source_target_pairs={{0,2},{2,4},{4,6},{6,8},{8,10},{10,12},{12,14},{1,3},{3,5},{5,7},{... | collective-permute-start | bytes 49160 | tf_op jit(solution)/shard_map/ppermute | solution.py:19
  109.1 1.3 copy-start.81
  110.0 2.2 copy-start.62
  117.9 6.0 %collective-permute-start.16 = (f32[2,16,1,128]{3,1,2,0:T(8,128)S(1)}, f32[2,16,1,128]{3,1,2,0:T(8,128)S(1)}, u32[]{:S(2)}, u32[]{:S(2)}) collective-permute-start(f32[2,16,1,128]{3,1,2,0:T(8,128)S(1)} %bitcast.589), channel_id=1, source_target_pairs={{1,0},{3,2},{5,4},{7,6},{9,8},{11,10},{13,12},{15,14},{17,16},{19,... | collective-permute-start | bytes 49160 | tf_op jit(solution)/shard_map/ppermute | solution.py:19
  119.3 5.5 %collective-permute-start.17 = (f32[2,1,16,128]{3,2,1,0:T(8,128)S(1)}, f32[2,1,16,128]{3,2,1,0:T(8,128)S(1)}, u32[]{:S(2)}, u32[]{:S(2)}) collective-permute-start(f32[2,1,16,128]{3,2,1,0:T(8,128)S(1)} %slice.1440), channel_id=1, source_target_pairs={{2,0},{4,2},{6,4},{8,6},{10,8},{12,10},{14,12},{3,1},{5,3},{7,5},{... | collective-permute-start | bytes 49160 | tf_op jit(solution)/shard_map/ppermute | solution.py:19
  126.2 9.8 %collective-permute-start.18 = (f32[2,16,1,128]{3,1,2,0:T(8,128)S(1)}, f32[2,16,1,128]{3,1,2,0:T(8,128)S(1)}, u32[]{:S(2)}, u32[]{:S(2)}) collective-permute-start(f32[2,16,1,128]{3,1,2,0:T(8,128)S(1)} %bitcast.596), channel_id=1, source_target_pairs={{0,1},{2,3},{4,5},{6,7},{8,9},{10,11},{12,13},{14,15},{16,17},{18,... | collective-permute-start | bytes 49160 | tf_op jit(solution)/shard_map/ppermute | solution.py:19
  132.3 4.5 %collective-permute-start.19 = (f32[2,1,16,128]{3,2,1,0:T(8,128)S(1)}, f32[2,1,16,128]{3,2,1,0:T(8,128)S(1)}, u32[]{:S(2)}, u32[]{:S(2)}) collective-permute-start(f32[2,1,16,128]{3,2,1,0:T(8,128)S(1)} %slice.1453), channel_id=1, source_target_pairs={{0,2},{2,4},{4,6},{6,8},{8,10},{10,12},{12,14},{1,3},{3,5},{5,7},{... | collective-permute-start | bytes 49160 | tf_op jit(solution)/shard_map/ppermute | solution.py:19
  143.8 6.0 %collective-permute-start.20 = (f32[2,16,1,128]{3,1,2,0:T(8,128)S(1)}, f32[2,16,1,128]{3,1,2,0:T(8,128)S(1)}, u32[]{:S(2)}, u32[]{:S(2)}) collective-permute-start(f32[2,16,1,128]{3,1,2,0:T(8,128)S(1)} %bitcast.590), channel_id=1, source_target_pairs={{1,0},{3,2},{5,4},{7,6},{9,8},{11,10},{13,12},{15,14},{17,16},{19,... | collective-permute-start | bytes 49160 | tf_op jit(solution)/shard_map/ppermute | solution.py:19
  145.2 4.7 %collective-permute-start.21 = (f32[2,1,16,128]{3,2,1,0:T(8,128)S(1)}, f32[2,1,16,128]{3,2,1,0:T(8,128)S(1)}, u32[]{:S(2)}, u32[]{:S(2)}) collective-permute-start(f32[2,1,16,128]{3,2,1,0:T(8,128)S(1)} %slice.1473), channel_id=1, source_target_pairs={{2,0},{4,2},{6,4},{8,6},{10,8},{12,10},{14,12},{3,1},{5,3},{7,5},{... | collective-permute-start | bytes 49160 | tf_op jit(solution)/shard_map/ppermute | solution.py:19
  150.1 1.3 copy-start.5
  151.5 9.8 %collective-permute-start.22 = (f32[2,16,1,128]{3,1,2,0:T(8,128)S(1)}, f32[2,16,1,128]{3,1,2,0:T(8,128)S(1)}, u32[]{:S(2)}, u32[]{:S(2)}) collective-permute-start(f32[2,16,1,128]{3,1,2,0:T(8,128)S(1)} %bitcast.597), channel_id=1, source_target_pairs={{0,1},{2,3},{4,5},{6,7},{8,9},{10,11},{12,13},{14,15},{16,17},{18,... | collective-permute-start | bytes 49160 | tf_op jit(solution)/shard_map/ppermute | solution.py:19
  157.7 4.5 %collective-permute-start.23 = (f32[2,1,16,128]{3,2,1,0:T(8,128)S(1)}, f32[2,1,16,128]{3,2,1,0:T(8,128)S(1)}, u32[]{:S(2)}, u32[]{:S(2)}) collective-permute-start(f32[2,1,16,128]{3,2,1,0:T(8,128)S(1)} %slice.1486), channel_id=1, source_target_pairs={{0,2},{2,4},{4,6},{6,8},{8,10},{10,12},{12,14},{1,3},{3,5},{5,7},{... | collective-permute-start | bytes 49160 | tf_op jit(solution)/shard_map/ppermute | solution.py:19
  170.8 6.0 %collective-permute-start.24 = (f32[2,16,1,128]{3,1,2,0:T(8,128)S(1)}, f32[2,16,1,128]{3,1,2,0:T(8,128)S(1)}, u32[]{:S(2)}, u32[]{:S(2)}) collective-permute-start(f32[2,16,1,128]{3,1,2,0:T(8,128)S(1)} %bitcast.591), channel_id=1, source_target_pairs={{1,0},{3,2},{5,4},{7,6},{9,8},{11,10},{13,12},{15,14},{17,16},{19,... | collective-permute-start | bytes 49160 | tf_op jit(solution)/shard_map/ppermute | solution.py:19
  172.2 5.0 %collective-permute-start.25 = (f32[2,1,16,128]{3,2,1,0:T(8,128)S(1)}, f32[2,1,16,128]{3,2,1,0:T(8,128)S(1)}, u32[]{:S(2)}, u32[]{:S(2)}) collective-permute-start(f32[2,1,16,128]{3,2,1,0:T(8,128)S(1)} %slice.1504), channel_id=1, source_target_pairs={{2,0},{4,2},{6,4},{8,6},{10,8},{12,10},{14,12},{3,1},{5,3},{7,5},{... | collective-permute-start | bytes 49160 | tf_op jit(solution)/shard_map/ppermute | solution.py:19
  177.5 1.3 copy-start.39
  177.6 1.3 copy-start.50
  177.6 1.3 copy-start.52
  178.9 9.8 %collective-permute-start.26 = (f32[2,16,1,128]{3,1,2,0:T(8,128)S(1)}, f32[2,16,1,128]{3,1,2,0:T(8,128)S(1)}, u32[]{:S(2)}, u32[]{:S(2)}) collective-permute-start(f32[2,16,1,128]{3,1,2,0:T(8,128)S(1)} %bitcast.598), channel_id=1, source_target_pairs={{0,1},{2,3},{4,5},{6,7},{8,9},{10,11},{12,13},{14,15},{16,17},{18,... | collective-permute-start | bytes 49160 | tf_op jit(solution)/shard_map/ppermute | solution.py:19
  185.1 4.5 %collective-permute-start.27 = (f32[2,1,16,128]{3,2,1,0:T(8,128)S(1)}, f32[2,1,16,128]{3,2,1,0:T(8,128)S(1)}, u32[]{:S(2)}, u32[]{:S(2)}) collective-permute-start(f32[2,1,16,128]{3,2,1,0:T(8,128)S(1)} %slice.1517), channel_id=1, source_target_pairs={{0,2},{2,4},{4,6},{6,8},{8,10},{10,12},{12,14},{1,3},{3,5},{5,7},{... | collective-permute-start | bytes 49160 | tf_op jit(solution)/shard_map/ppermute | solution.py:19
  198.3 6.0 %collective-permute-start.28 = (f32[2,16,1,128]{3,2,1,0:T(1,128)S(1)}, f32[2,16,1,128]{3,2,1,0:T(1,128)S(1)}, u32[]{:S(2)}, u32[]{:S(2)}) collective-permute-start(f32[2,16,1,128]{3,2,1,0:T(1,128)S(1)} %slice.1285), channel_id=1, source_target_pairs={{1,0},{3,2},{5,4},{7,6},{9,8},{11,10},{13,12},{15,14},{17,16},{19,... | collective-permute-start | bytes 49160 | tf_op jit(solution)/shard_map/ppermute | solution.py:19
  199.7 4.9 %collective-permute-start.29 = (f32[2,1,16,128]{3,2,1,0:T(8,128)S(1)}, f32[2,1,16,128]{3,2,1,0:T(8,128)S(1)}, u32[]{:S(2)}, u32[]{:S(2)}) collective-permute-start(f32[2,1,16,128]{3,2,1,0:T(8,128)S(1)} %slice.1535), channel_id=1, source_target_pairs={{2,0},{4,2},{6,4},{8,6},{10,8},{12,10},{14,12},{3,1},{5,3},{7,5},{... | collective-permute-start | bytes 49160 | tf_op jit(solution)/shard_map/ppermute | solution.py:19
  204.7 1.2 copy-start.7
  204.9 1.3 copy-start.51
  206.4 9.6 %collective-permute-start.30 = (f32[2,16,1,128]{3,1,2,0:T(8,128)S(1)}, f32[2,16,1,128]{3,1,2,0:T(8,128)S(1)}, u32[]{:S(2)}, u32[]{:S(2)}) collective-permute-start(f32[2,16,1,128]{3,1,2,0:T(8,128)S(1)} %bitcast.599), channel_id=1, source_target_pairs={{0,1},{2,3},{4,5},{6,7},{8,9},{10,11},{12,13},{14,15},{16,17},{18,... | collective-permute-start | bytes 49160 | tf_op jit(solution)/shard_map/ppermute | solution.py:19
  212.3 4.5 %collective-permute-start.31 = (f32[2,1,16,128]{3,2,1,0:T(8,128)S(1)}, f32[2,1,16,128]{3,2,1,0:T(8,128)S(1)}, u32[]{:S(2)}, u32[]{:S(2)}) collective-permute-start(f32[2,1,16,128]{3,2,1,0:T(8,128)S(1)} %slice.1548), channel_id=1, source_target_pairs={{0,2},{2,4},{4,6},{6,8},{8,10},{10,12},{12,14},{1,3},{3,5},{5,7},{... | collective-permute-start | bytes 49160 | tf_op jit(solution)/shard_map/ppermute | solution.py:19
  (67 other events, 65.3 us)
Sparse Core Ops, SparseCore 0:
  220.1 75.7 reduce-scatter.1
